TPU v7x, 32 devices: a whole 2x2x4 slice. The times are simulated.
32 devices in a mesh: mode: 8 (over z, y), space: 4 (over x, core).
Axes of the slice: x: 2, y: 2, z: 4, core: 2. Of those that a mesh axis runs over, the one named last changes fastest.
Arguments:
- modes: bfloat16 [3, 256, 16, 4, 128], P(None, 'mode', 'space'), may hold values from -6 to 6
- weights: float32 [16, 4, 128], P('space'), may hold values from 0.001275776 to 0.031894397
- plan: int32 [3], replicated, may hold values from 0 to 7, as said below
Outputs:
- convection: float32 [128, 32, 256], P('space', None, 'mode')
Inputs may be any that keep to these rules, and one draw needn't show every extreme that they name: plan[0] is 256 / 32 - 1, the last aligned block of 32 modes; plan[1] to plan[2] are distinct indices of aligned panels of 64 modes, below 256 / 64.
All inputs are finite; a program needn't handle non-finite values.
Results may differ from a plain program's by a relative error of at most 0.0041.
Values may be sent and summed in bfloat16 or wider, within the bound.
A program may use at most 128 MiB of HBM per device.

v0:
```python
import functools

import jax
import jax.numpy as jnp
from jax import lax
from jax.experimental import pallas as pl
from jax.experimental.pallas import tpu as pltpu
from jax.sharding import PartitionSpec as P

PANEL = 64
NPANEL = 2
SKEW = 3
TAIL = 4
LEAD = 2
MESH = pl.DeviceIdType.MESH
F32 = jnp.float32
BF16 = jnp.bfloat16


def kernel(dims, plan_ref, modes_ref, weights_ref, out_ref,
           ext, advb, up_in, dn_in, up_out, dn_out, tests, advf, vals, wts, acc, tot, stage, rs_in,
           halo_send, halo_recv, up_send, up_recv, dn_send, dn_recv, y_send, y_recv,
           ad_send, ay_send, adv_recv, rs_send, rs_recv):
    panels, spaces, cy, own_rows = dims
    chunks, _, nm, lanes = modes_ref.shape
    nx = weights_ref.shape[0]
    comps, cells = chunks // nx, nx * cy
    pairs = cells // 2
    quarter = pairs // 2
    last = panels - 1
    mode = lax.axis_index("mode")
    p = mode // 2
    q = lax.rem(mode, 2)
    me = lax.axis_index("space")
    partner = p * 2 + (1 - q)
    below = lax.rem(p + panels - 1, panels) * 2 + q
    above = lax.rem(p + 1, panels) * 2 + q
    right = lax.rem(me + 1, spaces)
    left = lax.rem(me + spaces - 1, spaces)
    is_src = jnp.logical_and(p == last, q == 1)
    not_src = jnp.logical_or(p < last, q == 0)

    barrier = pltpu.get_barrier_semaphore()
    pl.semaphore_signal(barrier, inc=1, device_id={"mode": partner}, device_id_type=MESH)

    @pl.when(p > 0)
    def _():
        pl.semaphore_signal(barrier, inc=1, device_id={"mode": below}, device_id_type=MESH)

    @pl.when(p < last)
    def _():
        pl.semaphore_signal(barrier, inc=1, device_id={"mode": above}, device_id_type=MESH)

    for d in range(1, spaces):
        pl.semaphore_signal(barrier, inc=1, device_id={"space": lax.rem(me + d, spaces)}, device_id_type=MESH)

    for m in range(chunks):
        first = cy * (1 + m % nx)
        ext[m // nx, first : first + cy] = modes_ref[m]

    @pl.when(is_src)
    def _():
        for a in range(pairs):
            for c in range(comps):
                at = 2 * a % cy
                advb[a, c] = modes_ref[c * nx + 2 * a // cy, at : at + 2]

    @pl.when(p == 0)
    def _():
        for m in range(chunks):
            for t in range(NPANEL):
                up_in[m, t] = modes_ref[m]

    @pl.when(p == last)
    def _():
        for m in range(chunks):
            for t in range(NPANEL):
                dn_in[m, t] = modes_ref[m]

    pl.semaphore_wait(barrier, spaces + (p > 0).astype(jnp.int32) + (p < last).astype(jnp.int32))

    def copy_adv_down(a):
        return pltpu.make_async_remote_copy(
            src_ref=advb.at[q * quarter + a], dst_ref=advb.at[q * quarter + a],
            send_sem=ad_send.at[a], recv_sem=adv_recv.at[q * quarter + a],
            device_id={"mode": below}, device_id_type=MESH)

    def copy_adv_side(x):
        return pltpu.make_async_remote_copy(
            src_ref=advb.at[x], dst_ref=advb.at[x],
            send_sem=ay_send.at[x], recv_sem=adv_recv.at[x],
            device_id={"mode": partner}, device_id_type=MESH)

    def copy_up(m):
        return pltpu.make_async_remote_copy(
            src_ref=up_out.at[m], dst_ref=up_in.at[m], send_sem=up_send.at[m], recv_sem=up_recv.at[m],
            device_id={"mode": above}, device_id_type=MESH)

    def copy_down(m):
        return pltpu.make_async_remote_copy(
            src_ref=dn_out.at[m], dst_ref=dn_in.at[m], send_sem=dn_send.at[m], recv_sem=dn_recv.at[m],
            device_id={"mode": below}, device_id_type=MESH)

    def copy_side(m):
        return pltpu.make_async_remote_copy(
            src_ref=tests.at[m, q], dst_ref=tests.at[m, q], send_sem=y_send.at[m], recv_sem=y_recv.at[m],
            device_id={"mode": partner}, device_id_type=MESH)

    @pl.when(is_src)
    def _():
        for a in range(pairs):
            copy_adv_side(a).start()

    halos = []
    for c in range(comps):
        for k, (plane, at, peer) in enumerate(((nx - 1, 0, right), (0, cells + cy, left))):
            halos.append(pltpu.make_async_remote_copy(
                src_ref=modes_ref.at[c * nx + plane], dst_ref=ext.at[c, pl.ds(at, cy)],
                send_sem=halo_send.at[c, k], recv_sem=halo_recv.at[c, k],
                device_id={"space": peer}, device_id_type=MESH))
    for halo in halos:
        halo.start()

    def values_of(xp):
        adv_at = advb.at[xp]
        for e in range(2):
            xy = 2 * xp + e
            x = lax.div(xp, cy // 2)
            y = xy - x * cy
            y_next = cy + x * cy + lax.rem(y + 1, cy)
            y_prev = cy + x * cy + lax.rem(y + cy - 1, cy)
            for d in range(3):
                advf[e, d] = adv_at[d, e].astype(F32)
            grads = []
            for c in range(comps):
                center = ext[c, xy + cy].astype(F32)
                gx = 0.5 * (ext[c, xy + 2 * cy].astype(F32) - ext[c, xy].astype(F32))
                gy = 0.5 * (ext[c, y_next].astype(F32) - ext[c, y_prev].astype(F32))
                gz = 0.5 * (pltpu.roll(center, lanes - 1, 1) - pltpu.roll(center, 1, 1))
                grads.append((gx, gy, gz))

            def row(j, carry):
                rows = [jnp.broadcast_to(advf[e, d, pl.ds(j, 1), :], (nm, lanes)) for d in range(3)]
                for c in range(comps):
                    value = rows[0] * grads[c][0] + rows[1] * grads[c][1] + rows[2] * grads[c][2]
                    start = pl.multiple_of(j * nm, nm)
                    vals[c * pairs + xp, pl.ds(start, nm), e * lanes : (e + 1) * lanes] = value.astype(BF16)
                return carry

            lax.fori_loop(0, nm, row, 0, unroll=4)

    def gemm(m):
        plane = lax.rem(m, nx)
        total = None
        for k in range(cy // 2):
            for e in range(2):
                weight = weights_ref[plane, 2 * k + e : 2 * k + e + 1, :]
                for t in range(NPANEL):
                    for s in range(2):
                        raw = tests[m, s, t, 2 * k + e].astype(F32)
                        r = (t * 2 + s) * nm
                        wts[k, r : r + nm, e * lanes : (e + 1) * lanes] = (weight * raw).astype(BF16)
            part = lax.dot_general(vals[m * (cy // 2) + k], wts[k], (((1,), (1,)), ((), ())), preferred_element_type=F32)
            total = part if total is None else total + part
        acc[...] += total

    off_up = SKEW * p
    off_adv = SKEW * (last - p)
    off_down = quarter + off_adv
    off_own = jnp.maximum(off_up, off_down)
    off_dot = off_own + TAIL
    ticks = quarter + SKEW * last + TAIL + chunks
    acc[...] = jnp.zeros_like(acc)

    def tick(step, carry):
        a = step - off_adv - LEAD

        @pl.when(jnp.logical_and(a >= 0, a < quarter))
        def _():
            @pl.when(not_src)
            def _():
                copy_adv_side(q * quarter + a).wait_recv()

            @pl.when(p > 0)
            def _():
                copy_adv_down(a).start()

            @pl.when(p < last)
            def _():
                copy_adv_side(q * quarter + a).start()

        mu = step - off_up

        @pl.when(jnp.logical_and(mu >= 0, mu < chunks))
        def _():
            @pl.when(p > 0)
            def _():
                copy_up(mu).wait_recv()

            @pl.when(p < last)
            def _():
                mine = modes_ref[mu]
                for t in range(NPANEL):
                    up_out[mu, t] = jnp.where(plan_ref[1 + t] == p, mine, up_in[mu, t])
                copy_up(mu).start()

        early = step - off_adv
        md = jnp.where(early < LEAD, early, step - off_down)

        @pl.when(jnp.logical_and(md >= jnp.where(early < LEAD, 0, LEAD), md < chunks))
        def _():
            @pl.when(p < last)
            def _():
                copy_down(md).wait_recv()

            @pl.when(p > 0)
            def _():
                mine = modes_ref[md]
                for t in range(NPANEL):
                    dn_out[md, t] = jnp.where(plan_ref[1 + t] == p, mine, dn_in[md, t])
                copy_down(md).start()

        mf = step - off_own

        @pl.when(jnp.logical_and(mf >= 0, mf < chunks))
        def _():
            mine = modes_ref[mf]
            for t in range(NPANEL):
                owner = plan_ref[1 + t]
                got = jnp.where(owner < p, up_in[mf, t], dn_in[mf, t])
                tests[mf, q, t] = jnp.where(owner == p, mine, got)
            copy_side(mf).start()

        @pl.when(jnp.logical_and(a >= 0, a < pairs))
        def _():
            @pl.when(a == 0)
            def _():
                for halo in halos:
                    halo.wait_recv()

            xp = lax.rem(q * quarter + a, pairs)

            @pl.when(jnp.logical_and(a >= quarter, not_src))
            def _():
                copy_adv_side(xp).wait_recv()

            values_of(xp)

        mg = step - off_dot

        @pl.when(jnp.logical_and(mg >= 0, mg < chunks))
        def _():
            copy_side(mg).wait_recv()
            gemm(mg)

        return carry

    lax.fori_loop(0, ticks, tick, 0)

    for jt in range(nm * nm // lanes):
        turned = acc[jt * lanes : (jt + 1) * lanes, :].T
        for s in range(spaces):
            piece = turned[s * own_rows : (s + 1) * own_rows]
            tot[s, :, jt * lanes : (jt + 1) * lanes] = piece
            stage[s, :, jt * lanes : (jt + 1) * lanes] = piece.astype(BF16)

    copies = []
    for d in range(1, spaces):
        peer = lax.rem(me + d, spaces)
        copies.append(pltpu.make_async_remote_copy(
            src_ref=stage.at[peer], dst_ref=rs_in.at[d - 1], send_sem=rs_send.at[d - 1],
            recv_sem=rs_recv.at[d - 1], device_id={"space": peer}, device_id_type=MESH))
    for copy in copies:
        copy.start()

    for halo in halos:
        halo.wait_send()

    @pl.when(is_src)
    def _():
        for a in range(pairs):
            copy_adv_side(a).wait_send()

    @pl.when(p < last)
    def _():
        def done(a, carry):
            copy_adv_side(q * quarter + a).wait_send()
            return carry
        lax.fori_loop(0, quarter, done, 0)

        def done_up(m, carry):
            copy_up(m).wait_send()
            return carry
        lax.fori_loop(0, chunks, done_up, 0)

    @pl.when(p > 0)
    def _():
        def done(a, carry):
            copy_adv_down(a).wait_send()
            return carry
        lax.fori_loop(0, quarter, done, 0)

        def done_down(m, carry):
            copy_down(m).wait_send()
            return carry
        lax.fori_loop(0, chunks, done_down, 0)

    def done_side(m, carry):
        copy_side(m).wait_send()
        return carry

    lax.fori_loop(0, chunks, done_side, 0)

    total = tot[me]
    for d, copy in enumerate(copies):
        copy.wait_recv()
        total = total + rs_in[d].astype(F32)
    out_ref[...] = total
    for copy in copies:
        copy.wait_send()


def solution(mesh):
    nmode, spaces = mesh.shape["mode"], mesh.shape["space"]

    def local(modes, weights, plan):
        comps, nm, nx, cy, lanes = modes.shape
        cells = nx * cy
        assert PANEL == 2 * nm and nmode % 2 == 0
        test_count = NPANEL * PANEL
        own_rows = test_count // spaces
        turned = modes.transpose(0, 2, 3, 1, 4).reshape(comps * nx, cy, nm, lanes)
        pairs = cells // 2
        chunks = comps * nx
        quarter = pairs // 2
        vm = pl.BlockSpec(memory_space=pltpu.VMEM)
        chunk = (chunks, NPANEL, cy, nm, lanes)
        dma = pltpu.SemaphoreType.DMA
        out = pl.pallas_call(
            functools.partial(kernel, (nmode // 2, spaces, cy, own_rows)),
            out_shape=jax.ShapeDtypeStruct((own_rows, nm * nm), F32),
            in_specs=[pl.BlockSpec(memory_space=pltpu.SMEM), vm, vm],
            out_specs=vm,
            scratch_shapes=[
                pltpu.VMEM((comps, cells + 2 * cy, nm, lanes), BF16),
                pltpu.VMEM((pairs, comps, 2, nm, lanes), BF16),
                pltpu.VMEM(chunk, BF16), pltpu.VMEM(chunk, BF16), pltpu.VMEM(chunk, BF16), pltpu.VMEM(chunk, BF16),
                pltpu.VMEM((chunks, 2, NPANEL, cy, nm, lanes), BF16),
                pltpu.VMEM((2, comps, nm, lanes), F32),
                pltpu.VMEM((comps * pairs, nm * nm, 2 * lanes), BF16),
                pltpu.VMEM((cy // 2, test_count, 2 * lanes), BF16),
                pltpu.VMEM((nm * nm, test_count), F32),
                pltpu.VMEM((spaces, own_rows, nm * nm), F32),
                pltpu.VMEM((spaces, own_rows, nm * nm), BF16),
                pltpu.VMEM((spaces - 1, own_rows, nm * nm), BF16),
                dma((comps, 2)), dma((comps, 2)),
                dma((chunks,)), dma((chunks,)), dma((chunks,)), dma((chunks,)), dma((chunks,)), dma((chunks,)),
                dma((quarter,)), dma((pairs,)), dma((pairs,)),
                dma((spaces - 1,)), dma((spaces - 1,)),
            ],
            compiler_params=pltpu.CompilerParams(
                collective_id=0, has_side_effects=True, vmem_limit_bytes=48 * 1024 * 1024),
        )(plan, turned, weights)
        return out.reshape(own_rows, nm, nm)

    in_specs = (P(None, "mode", "space", None, None), P("space", None, None), P())
    return jax.shard_map(local, mesh=mesh, in_specs=in_specs, out_specs=P("space", None, "mode"), check_vma=False)
```

profile of v0, /device:TPU:0, one launch (start us, length us, event | category | flops | bytes accessed | tf_op | source)
XLA Modules:
  0.0 49.0 jit_solution(6411640815277063674)
XLA Ops:
  0.0 0.0 copy-start
  0.0 1.1 %copy.4 = bf16[3,4,4,32,128]{4,3,2,1,0:T(8,128)(2,1)S(1)} copy(bf16[3,4,4,32,128]{4,2,1,3,0:T(4,128)(2,1)} %bitcast.3) | data formatting | bytes 786432 | tf_op jit(solution)/shard_map/transpose | solution.py:332
  1.1 0.0 copy-start.1
  1.1 0.0 copy-done
  1.1 0.6 %copy-done.1 = s32[3]{0:T(128)S(1)} copy-done((s32[3]{0:T(128)S(1)}, s32[3]{0:T(128)}, u32[]{:S(2)}) %copy-start.1) | copy-done | bytes 36
  1.8 46.3 %shard_map.37 = f32[32,1024]{1,0:T(8,128)S(1)} custom-call(s32[3]{0:T(128)S(1)} %copy-done.1, bf16[12,4,32,128]{3,2,1,0:T(8,128)(2,1)S(1)} %bitcast.2, f32[4,4,128]{2,1,0:T(4,128)S(1)} %copy-done), custom_call_target="tpu_custom_call" | custom-call | tf_op jit(solution)/shard_map/pallas_call | solution.py:339
  48.1 1.0 %reshape.7 = f32[32,32,32]{2,1,0:T(8,128)} reshape(f32[32,1024]{1,0:T(8,128)S(1)} %shard_map.37) | data formatting | bytes 262144 | tf_op jit(solution)/shard_map/reshape | solution.py:364
Async XLA Ops:
  0.0 1.1 %copy-start = (f32[4,4,128]{2,1,0:T(4,128)S(1)}, f32[4,4,128]{2,1,0:T(4,128)}, u32[]{:S(2)}) copy-start(f32[4,4,128]{2,1,0:T(4,128)} %weights_ref.1) | copy-start | bytes 24580
  1.1 0.7 %copy-start.1 = (s32[3]{0:T(128)S(1)}, s32[3]{0:T(128)}, u32[]{:S(2)}) copy-start(s32[3]{0:T(128)} %plan_ref.1) | copy-start | bytes 40
where the time goes:
time: 49.2 us; the launch traced here: 49 us
  Pallas kernels  46.3 us (94%)
  local copies, waits for them, and re-layouts  2.72 us (6%)
    pallas_call x1, Pallas kernels, local(): pl.pallas_call(functools.partial(kernel, (nmode // 2, spaces, cy, own_row...  46.3 us
    transpose x1, local copies, waits for them, and re-layouts, local(): turned = modes.transpose(0, 2, 3, 1, 4).reshape(comps * nx, cy, nm, lanes)  1.11 us

commit v1 on v0

v1 whole, which is shorter than its diff:
```python
import functools

import jax
import jax.numpy as jnp
from jax import lax
from jax.experimental import pallas as pl
from jax.experimental.pallas import tpu as pltpu
from jax.sharding import PartitionSpec as P

PANEL = 64
NPANEL = 2
MESH = pl.DeviceIdType.MESH
F32 = jnp.float32
BF16 = jnp.bfloat16


def kernel(dims, plan_ref, x_ref, weights_ref, out_ref,
           pk, bd, gq, bq, wq, advf, wts, vals, acc, crx, own, xo, xi, zo, zi,
           z_send, z_recv, b_send, b_recv, y_send, y_recv, h_send, h_recv,
           c_send, c_recv, s_send, s_recv, r_send, r_recv):
    nmode, spaces = dims
    comps, nm, nx, cy, lanes = x_ref.shape
    own_rows = out_ref.shape[0]
    parts = cy
    width = lanes // parts
    units = nx * comps
    cols = nmode // parts
    half = spaces // 2
    per_panel = PANEL // nm
    mode = lax.axis_index("mode")
    me = lax.axis_index("space")
    zq = lax.rem(mode // 2, parts)
    col = (mode // (2 * parts)) * 2 + lax.rem(mode, 2)
    core = lax.rem(me, 2)
    row = me // 2
    adv_block = nmode - 1

    def member(c, z):
        return (c // 2) * (2 * parts) + z * 2 + lax.rem(c, 2)

    def to_mode(m):
        return {"device_id": {"mode": m}, "device_id_type": MESH}

    def to_space(s):
        return {"device_id": {"space": s}, "device_id_type": MESH}

    barrier = pltpu.get_barrier_semaphore()
    for d in range(1, parts):
        pl.semaphore_signal(barrier, inc=1, **to_mode(member(col, lax.rem(zq + d, parts))))
    for d in range(1, cols):
        pl.semaphore_signal(barrier, inc=1, **to_mode(member(lax.rem(col + d, cols), zq)))
    for d in range(1, spaces):
        pl.semaphore_signal(barrier, inc=1, **to_space(lax.rem(me + d, spaces)))

    lane = lax.broadcasted_iota(jnp.int32, (nm, lanes), 1)
    group, inner = lane // width, lax.rem(lane, width)

    def roll(v, shift):
        shift = shift % lanes
        return pltpu.roll(v, shift, 1) if shift else v

    edges = [jnp.zeros((nm, lanes), F32) for _ in range(parts)]
    for p in range(nx):
        for c in range(comps):
            u = p * comps + c
            rows = jnp.swapaxes(x_ref[c, :, p], 0, 1)
            rows = [rows[y].astype(F32) for y in range(cy)]
            packed = []
            for t in range(parts):
                v = roll(rows[0], -width * t)
                for y in range(1, cy):
                    v = jnp.where(group == y, roll(rows[y], width * (y - t)), v)
                packed.append(v)
                pk[t, u] = v.astype(BF16)
            for t in range(parts):
                low = roll(packed[(t - 1) % parts], 2 * u - width + 1)
                high = roll(packed[(t + 1) % parts], 2 * u + 1)
                edges[t] = jnp.where(inner == 2 * u, low, jnp.where(inner == 2 * u + 1, high, edges[t]))
    for t in range(parts):
        bd[t] = edges[t].astype(BF16)
    gq[mode, comps : comps + units] = pk[zq]
    bq[zq] = bd[zq]
    for p in range(nx):
        w = None
        for y in range(cy):
            line = jnp.broadcast_to(weights_ref[p, y : y + 1, :], (8, lanes))
            line = pltpu.roll(line, lax.rem(width * (y - zq + parts), lanes), 1)
            w = line if w is None else jnp.where(group[:8] == y, line, w)
        wq[p] = w

    pl.semaphore_wait(barrier, parts - 1 + cols - 1 + spaces - 1)

    def copy_z(d, p):
        t = lax.rem(zq + d, parts)
        return pltpu.make_async_remote_copy(
            src_ref=pk.at[t, pl.ds(p * comps, comps)], dst_ref=gq.at[mode, pl.ds((p + 1) * comps, comps)],
            send_sem=z_send.at[d - 1, p], recv_sem=z_recv.at[zq, p], **to_mode(member(col, t)))

    def got_z(z, p):
        m = member(col, z)
        return pltpu.make_async_remote_copy(
            src_ref=pk.at[0, pl.ds(p * comps, comps)], dst_ref=gq.at[m, pl.ds((p + 1) * comps, comps)],
            send_sem=z_send.at[0, p], recv_sem=z_recv.at[z, p], **to_mode(m))

    def copy_b(d):
        t = lax.rem(zq + d, parts)
        return pltpu.make_async_remote_copy(
            src_ref=bd.at[t], dst_ref=bq.at[zq],
            send_sem=b_send.at[d - 1], recv_sem=b_recv.at[zq], **to_mode(member(col, t)))

    def got_b(z):
        return pltpu.make_async_remote_copy(
            src_ref=bd.at[0], dst_ref=bq.at[z],
            send_sem=b_send.at[0], recv_sem=b_recv.at[z], **to_mode(member(col, z)))

    def copy_y(d, z, p):
        m = member(col, z)
        part = gq.at[m, pl.ds((p + 1) * comps, comps)]
        return pltpu.make_async_remote_copy(
            src_ref=part, dst_ref=part, send_sem=y_send.at[d - 1, z, p], recv_sem=y_recv.at[cols - d - 1, z, p],
            **to_mode(member(lax.rem(col + d, cols), zq)))

    def got_y(d, z, p):
        peer = lax.rem(col + d, cols)
        part = gq.at[member(peer, z), pl.ds((p + 1) * comps, comps)]
        return pltpu.make_async_remote_copy(
            src_ref=part, dst_ref=part, send_sem=y_send.at[d - 1, z, p], recv_sem=y_recv.at[d - 1, z, p],
            **to_mode(member(peer, zq)))

    def copy_h(z, side):
        m = member(col, z)
        first, there, peer = ((nx * comps, 0, me + 1), (comps, (nx + 1) * comps, me + spaces - 1))[side]
        return pltpu.make_async_remote_copy(
            src_ref=gq.at[m, pl.ds(first, comps)], dst_ref=gq.at[m, pl.ds(there, comps)],
            send_sem=h_send.at[z, side], recv_sem=h_recv.at[z, side], **to_space(lax.rem(peer, spaces)))

    def copy_c(n):
        return pltpu.make_async_remote_copy(
            src_ref=acc.at[n, 1 - core], dst_ref=crx.at[n],
            send_sem=c_send.at[n], recv_sem=c_recv.at[n], **to_space(row * 2 + 1 - core))

    def copy_s(n, d):
        peer = lax.rem(row + d, half)
        return pltpu.make_async_remote_copy(
            src_ref=xo.at[n, peer], dst_ref=xi.at[n, half - d - 1],
            send_sem=s_send.at[n, d - 1], recv_sem=s_recv.at[n, half - d - 1], **to_space(peer * 2 + core))

    def got_s(n, d):
        peer = lax.rem(row + d, half)
        return pltpu.make_async_remote_copy(
            src_ref=xo.at[n, peer], dst_ref=xi.at[n, d - 1],
            send_sem=s_send.at[n, d - 1], recv_sem=s_recv.at[n, d - 1], **to_space(peer * 2 + core))

    def copy_r(n):
        return pltpu.make_async_remote_copy(
            src_ref=zo.at[n], dst_ref=zi.at[n],
            send_sem=r_send.at[n], recv_sem=r_recv.at[n], **to_mode(member(col, lax.rem(zq + 1 + n, parts))))

    source = zq == parts - 1

    @pl.when(source)
    def _():
        for p in range(nx):
            for d in range(1, parts):
                copy_z(d, p).start()

    @pl.when(jnp.logical_not(source))
    def _():
        for d in range(1, parts):
            for p in range(nx):
                copy_z(d, p).start()

    for d in range(1, parts):
        copy_b(d).start()
    for p in range(nx):
        for d in range(1, cols):
            copy_y(d, zq, p).start()
    for side in range(2):
        copy_h(zq, side).start()

    def other(n):
        head = parts - 1 if n == 0 else lax.rem(zq - n + parts - 1, parts - 1)
        return jnp.where(source, parts - 2 - n, head)

    def forward(z):
        for p in range(nx):
            got_z(z, p).wait_recv()
            for d in range(1, cols):
                copy_y(d, z, p).start()
            if p == 0:
                copy_h(z, 1).start()
        copy_h(z, 0).start()

    def values_of(z):
        m = member(col, z)
        edge = bq[z].astype(F32)
        for side in range(2):
            copy_h(z, side).wait_recv()
        for p in range(nx):
            grads = []
            for c in range(comps):
                u = p * comps + c
                at = (p + 1) * comps + c
                center = gq[m, at].astype(F32)
                gx = 0.5 * (gq[m, at + comps].astype(F32) - gq[m, at - comps].astype(F32))
                gy = 0.5 * (roll(center, -width) - roll(center, width))
                after = jnp.where(inner == width - 1, roll(edge, width - 2 - 2 * u), roll(center, -1))
                before = jnp.where(inner == 0, roll(edge, -2 * u), roll(center, 1))
                grads.append((gx, gy, 0.5 * (after - before)))

            def line(j, carry):
                rows = [jnp.broadcast_to(advf[p, d, pl.ds(j, 1), :], (nm, lanes)) for d in range(3)]
                start = pl.multiple_of(j * nm, nm)
                for c in range(comps):
                    value = rows[0] * grads[c][0] + rows[1] * grads[c][1] + rows[2] * grads[c][2]
                    vals[z, p * comps + c, pl.ds(start, nm), :] = value.astype(BF16)
                return carry

            lax.fori_loop(0, nm, line, 0, unroll=4)

    forward(other(0))

    adv_rel = cols - 1 - col

    @pl.when(col != cols - 1)
    def _():
        for p in range(nx):
            got_y(adv_rel, parts - 1, p).wait_recv()

    for p in range(nx):
        for d in range(comps):
            advf[p, d] = gq[adv_block, (p + 1) * comps + d].astype(F32)

    values_of(zq)
    for n in range(1, parts - 1):
        forward(other(n))
        got_b(other(n - 1)).wait_recv()
        values_of(other(n - 1))
    got_b(other(parts - 2)).wait_recv()
    values_of(other(parts - 2))

    for d in range(1, cols):
        for z in range(parts):
            def rest(d=d, z=z):
                for p in range(nx):
                    got_y(d, z, p).wait_recv()
            if z == parts - 1:
                pl.when(adv_rel != d)(rest)
            else:
                rest()

    for u in range(units):
        weight = wq[u // comps, 0:1, :]
        for t in range(NPANEL):
            for r in range(per_panel):
                raw = gq[plan_ref[1 + t] * per_panel + r, comps + u].astype(F32)
                first = (t * per_panel + r) * nm
                wts[u, first : first + nm, :] = (weight * raw).astype(BF16)

    def gemm(n):
        z = lax.rem(zq + 1 + n, parts)
        left = jnp.concatenate([wts[u] for u in range(units)], axis=1)
        right = jnp.concatenate([vals[z, u] for u in range(units)], axis=1)
        part = lax.dot_general(left, right, (((1,), (1,)), ((), ())), preferred_element_type=F32)
        for s in range(spaces):
            acc[n, s % 2, s // 2] = part[s * own_rows : (s + 1) * own_rows]
        copy_c(n).start()

    def stage_s(n):
        copy_c(n).wait_recv()
        for h in range(half):
            xo[n, h] = (acc[n, core, h] + crx[n, h]).astype(BF16)
        own[n] = acc[n, core, row] + crx[n, row]
        for d in range(1, half):
            copy_s(n, d).start()

    def total(n):
        value = own[n]
        for d in range(1, half):
            got_s(n, d).wait_recv()
            value = value + xi[n, d - 1].astype(F32)
        return value

    def stage_r(n):
        zo[n] = total(n).astype(BF16)
        copy_r(n).start()

    for n in range(parts):
        gemm(n)
        if n >= 1:
            stage_s(n - 1)
        if n >= 2:
            stage_r(n - 2)
    stage_s(parts - 1)
    stage_r(parts - 2)

    result = total(parts - 1)
    for n in range(parts - 1):
        copy_r(n).wait_recv()
        result = result + zi[n].astype(F32)
    out_ref[...] = result

    for d in range(1, parts):
        for p in range(nx):
            copy_z(d, p).wait_send()
        copy_b(d).wait_send()
    for z in range(parts):
        for d in range(1, cols):
            for p in range(nx):
                copy_y(d, z, p).wait_send()
        for side in range(2):
            copy_h(z, side).wait_send()
    for n in range(parts):
        copy_c(n).wait_send()
        for d in range(1, half):
            copy_s(n, d).wait_send()
        if n < parts - 1:
            copy_r(n).wait_send()


def solution(mesh):
    nmode, spaces = mesh.shape["mode"], mesh.shape["space"]

    def local(modes, weights, plan):
        comps, nm, nx, cy, lanes = modes.shape
        parts, units = cy, comps * nx
        cols, half = nmode // parts, spaces // 2
        test_count = NPANEL * PANEL
        own_rows = test_count // spaces
        assert PANEL % nm == 0 and lanes % parts == 0 and 2 * units <= lanes // parts
        assert nmode % (2 * parts) == 0 and spaces % 2 == 0
        vm = pl.BlockSpec(memory_space=pltpu.VMEM)
        dma = pltpu.SemaphoreType.DMA
        piece = (own_rows, nm * nm)
        pairs = max(half - 1, 1)
        out = pl.pallas_call(
            functools.partial(kernel, (nmode, spaces)),
            out_shape=jax.ShapeDtypeStruct(piece, F32),
            in_specs=[pl.BlockSpec(memory_space=pltpu.SMEM), vm, vm],
            out_specs=vm,
            scratch_shapes=[
                pltpu.VMEM((parts, units, nm, lanes), BF16),
                pltpu.VMEM((parts, nm, lanes), BF16),
                pltpu.VMEM((nmode, units + 2 * comps, nm, lanes), BF16),
                pltpu.VMEM((parts, nm, lanes), BF16),
                pltpu.VMEM((nx, 8, lanes), F32),
                pltpu.VMEM((nx, comps, nm, lanes), F32),
                pltpu.VMEM((units, test_count, lanes), BF16),
                pltpu.VMEM((parts, units, nm * nm, lanes), BF16),
                pltpu.VMEM((parts, 2, half) + piece, F32),
                pltpu.VMEM((parts, half) + piece, F32),
                pltpu.VMEM((parts,) + piece, F32),
                pltpu.VMEM((parts, half) + piece, BF16),
                pltpu.VMEM((parts, pairs) + piece, BF16),
                pltpu.VMEM((parts - 1,) + piece, BF16),
                pltpu.VMEM((parts - 1,) + piece, BF16),
                dma((parts - 1, nx)), dma((parts, nx)), dma((parts - 1,)), dma((parts,)),
                dma((cols - 1, parts, nx)), dma((cols - 1, parts, nx)), dma((parts, 2)), dma((parts, 2)),
                dma((parts,)), dma((parts,)), dma((parts, pairs)), dma((parts, pairs)),
                dma((parts - 1,)), dma((parts - 1,)),
            ],
            compiler_params=pltpu.CompilerParams(
                collective_id=0, has_side_effects=True, vmem_limit_bytes=56 * 1024 * 1024),
        )(plan, modes, weights)
        return out.reshape(own_rows, nm, nm)

    in_specs = (P(None, "mode", "space", None, None), P("space", None, None), P())
    return jax.shard_map(local, mesh=mesh, in_specs=in_specs, out_specs=P("space", None, "mode"), check_vma=False)
```

time: 49.2 us -> 43.8 us (0.89)
  Pallas kernels: 46.3 us -> 41.8 us
  local copies, waits for them, and re-layouts: 2.72 us -> 1.87 us
    pallas_call x1, Pallas kernels: 46.3 us -> 41.8 us  [local(): pl.pallas_call(functools.partial(kernel, (nmode, spaces)), out_shape=jax....]
    transpose x1 -> x0, local copies, waits for them, and re-layouts: 1.11 us -> none  [local(): turned = modes.transpose(0, 2, 3, 1, 4).reshape(comps * nx, cy, nm, lanes)]
    reshape x1, local copies, waits for them, and re-layouts: 0.97 us -> 1.87 us  [local(): return out.reshape(own_rows, nm, nm)]
    unnamed x4 -> x0, local copies, waits for them, and re-layouts: 0.64 us -> none
where the time goes in v1:
time: 43.8 us; the launch traced here: 43.7 us
  Pallas kernels  41.8 us (95%)
  local copies, waits for them, and re-layouts  1.87 us (4%)
    pallas_call x1, Pallas kernels, local(): pl.pallas_call(functools.partial(kernel, (nmode, spaces)), out_shape=jax....  41.8 us
    reshape x1, local copies, waits for them, and re-layouts, local(): return out.reshape(own_rows, nm, nm)  1.87 us

profile of v1, /device:TPU:0, one launch (start us, length us, event | category | flops | bytes accessed | tf_op | source)
XLA Modules:
  0.0 43.7 jit_solution(9041715290457201829)
XLA Ops:
  0.0 41.8 %shard_map.37 = f32[32,1024]{1,0:T(8,128)} custom-call(s32[3]{0:T(128)} %plan_ref.1, bf16[3,32,4,4,128]{4,3,2,1,0:T(4,128)(2,1)} %x_ref.1, f32[4,4,128]{2,1,0:T(4,128)} %weights_ref.1), custom_call_target="tpu_custom_call" | custom-call | tf_op jit(solution)/shard_map/pallas_call | solution.py:336
  41.8 1.9 %reshape.3 = f32[32,32,32]{2,1,0:T(8,128)} reshape(f32[32,1024]{1,0:T(8,128)} %shard_map.37) | data formatting | bytes 262144 | tf_op jit(solution)/shard_map/reshape | solution.py:365

commit v2 on v1

v2 whole, which is shorter than its diff:
```python
import functools

import jax
import jax.numpy as jnp
from jax import lax
from jax.experimental import pallas as pl
from jax.experimental.pallas import tpu as pltpu
from jax.sharding import PartitionSpec as P

PANEL = 64
NPANEL = 2
SPLIT = 2
LAG_S = 2
LAG_R = 5
MESH = pl.DeviceIdType.MESH
F32 = jnp.float32
BF16 = jnp.bfloat16


def kernel(dims, plan_ref, x_ref, weights_ref, out_ref,
           pk, bd, gq, bq, wq, advf, wts, vals, acc, cbo, crx, own, xo, xi, zo, zi, fin,
           z_send, z_recv, b_send, b_recv, y_send, y_recv, h_send, h_recv,
           c_send, c_recv, s_send, s_recv, r_send, r_recv):
    nmode, spaces = dims
    comps, nm, nx, cy, lanes = x_ref.shape
    own_rows = out_ref.shape[0] // nm
    parts = cy
    width = lanes // parts
    units = nx * comps
    cols = nmode // parts
    half = spaces // 2
    per_panel = PANEL // nm
    mode = lax.axis_index("mode")
    me = lax.axis_index("space")
    zq = lax.rem(mode // 2, parts)
    col = (mode // (2 * parts)) * 2 + lax.rem(mode, 2)
    core = lax.rem(me, 2)
    row = me // 2
    adv_block = nmode - 1
    planes = list(range(1, nx - 1)) + [0, nx - 1]
    steps = parts * SPLIT
    span = nm * nm // SPLIT

    def member(c, z):
        return (c // 2) * (2 * parts) + z * 2 + lax.rem(c, 2)

    def to_mode(m):
        return {"device_id": {"mode": m}, "device_id_type": MESH}

    def to_space(s):
        return {"device_id": {"space": s}, "device_id_type": MESH}

    barrier = pltpu.get_barrier_semaphore()
    for d in range(1, parts):
        pl.semaphore_signal(barrier, inc=1, **to_mode(member(col, lax.rem(zq + d, parts))))
    for d in range(1, cols):
        pl.semaphore_signal(barrier, inc=1, **to_mode(member(lax.rem(col + d, cols), zq)))
    for d in range(1, spaces):
        pl.semaphore_signal(barrier, inc=1, **to_space(lax.rem(me + d, spaces)))

    lane = lax.broadcasted_iota(jnp.int32, (nm, lanes), 1)
    group, inner = lane // width, lax.rem(lane, width)

    def roll(v, shift):
        shift = shift % lanes
        return pltpu.roll(v, shift, 1) if shift else v

    for p in range(nx):
        for c in range(comps):
            u = p * comps + c
            rows = jnp.swapaxes(x_ref[c, :, p], 0, 1)
            rows = [rows[y].astype(F32) for y in range(cy)]
            for t in range(parts):
                v = roll(rows[0], -width * t)
                for y in range(1, cy):
                    v = jnp.where(group == y, roll(rows[y], width * (y - t)), v)
                pk[t, u] = v.astype(BF16)
    gq[mode, comps : comps + units] = pk[zq]
    for p in range(nx):
        w = None
        for y in range(cy):
            line = jnp.broadcast_to(weights_ref[p, y : y + 1, :], (8, lanes))
            line = pltpu.roll(line, lax.rem(width * (y - zq + parts), lanes), 1)
            w = line if w is None else jnp.where(group[:8] == y, line, w)
        wq[p] = w

    pl.semaphore_wait(barrier, parts - 1 + cols - 1 + spaces - 1)

    def copy_z(t, p):
        return pltpu.make_async_remote_copy(
            src_ref=pk.at[t, pl.ds(p * comps, comps)], dst_ref=gq.at[mode, pl.ds((p + 1) * comps, comps)],
            send_sem=z_send.at[t, p], recv_sem=z_recv.at[zq, p], **to_mode(member(col, t)))

    def got_z(z, p):
        m = member(col, z)
        return pltpu.make_async_remote_copy(
            src_ref=pk.at[0, pl.ds(p * comps, comps)], dst_ref=gq.at[m, pl.ds((p + 1) * comps, comps)],
            send_sem=z_send.at[0, p], recv_sem=z_recv.at[z, p], **to_mode(m))

    def copy_b(d):
        t = lax.rem(zq + d, parts)
        return pltpu.make_async_remote_copy(
            src_ref=bd.at[t], dst_ref=bq.at[zq],
            send_sem=b_send.at[d - 1], recv_sem=b_recv.at[zq], **to_mode(member(col, t)))

    def got_b(z):
        return pltpu.make_async_remote_copy(
            src_ref=bd.at[0], dst_ref=bq.at[z],
            send_sem=b_send.at[0], recv_sem=b_recv.at[z], **to_mode(member(col, z)))

    def copy_y(d, z, p):
        m = member(col, z)
        part = gq.at[m, pl.ds((p + 1) * comps, comps)]
        return pltpu.make_async_remote_copy(
            src_ref=part, dst_ref=part, send_sem=y_send.at[d - 1, z, p], recv_sem=y_recv.at[cols - d - 1, z, p],
            **to_mode(member(lax.rem(col + d, cols), zq)))

    def got_y(d, z, p):
        peer = lax.rem(col + d, cols)
        part = gq.at[member(peer, z), pl.ds((p + 1) * comps, comps)]
        return pltpu.make_async_remote_copy(
            src_ref=part, dst_ref=part, send_sem=y_send.at[d - 1, z, p], recv_sem=y_recv.at[d - 1, z, p],
            **to_mode(member(peer, zq)))

    def copy_h(z, side):
        m = member(col, z)
        first, there, peer = ((nx * comps, 0, me + 1), (comps, (nx + 1) * comps, me + spaces - 1))[side]
        return pltpu.make_async_remote_copy(
            src_ref=gq.at[m, pl.ds(first, comps)], dst_ref=gq.at[m, pl.ds(there, comps)],
            send_sem=h_send.at[z, side], recv_sem=h_recv.at[z, side], **to_space(lax.rem(peer, spaces)))

    def copy_c(n):
        return pltpu.make_async_remote_copy(
            src_ref=cbo.at[n], dst_ref=crx.at[n],
            send_sem=c_send.at[n], recv_sem=c_recv.at[n], **to_space(row * 2 + 1 - core))

    def copy_s(n, d):
        peer = lax.rem(row + d, half)
        return pltpu.make_async_remote_copy(
            src_ref=xo.at[n, peer], dst_ref=xi.at[n, half - d - 1],
            send_sem=s_send.at[n, d - 1], recv_sem=s_recv.at[n, half - d - 1], **to_space(peer * 2 + core))

    def got_s(n, d):
        peer = lax.rem(row + d, half)
        return pltpu.make_async_remote_copy(
            src_ref=xo.at[n, peer], dst_ref=xi.at[n, d - 1],
            send_sem=s_send.at[n, d - 1], recv_sem=s_recv.at[n, d - 1], **to_space(peer * 2 + core))

    def copy_r(n):
        return pltpu.make_async_remote_copy(
            src_ref=zo.at[n], dst_ref=zi.at[n],
            send_sem=r_send.at[n], recv_sem=r_recv.at[n], **to_mode(member(col, lax.rem(zq + 1 + n // SPLIT, parts))))

    source = zq == parts - 1

    @pl.when(source)
    def _():
        for p in planes:
            for t in range(parts - 1):
                copy_z(t, p).start()

    for t in range(1, parts):
        @pl.when(t > zq)
        def _():
            for p in planes:
                copy_z(t, p).start()

    for p in planes:
        for d in range(1, cols):
            copy_y(d, zq, p).start()
    for side in range(2):
        copy_h(zq, side).start()

    for t in range(parts):
        edge = jnp.zeros((nm, lanes), F32)
        for u in range(units):
            low = roll(pk[(t - 1) % parts, u].astype(F32), 2 * u - width + 1)
            high = roll(pk[(t + 1) % parts, u].astype(F32), 2 * u + 1)
            edge = jnp.where(inner == 2 * u, low, jnp.where(inner == 2 * u + 1, high, edge))
        bd[t] = edge.astype(BF16)
    bq[zq] = bd[zq]
    for d in range(1, parts):
        copy_b(d).start()

    tail = zq == 0

    def other(n):
        head = parts - 1 if n == 0 else lax.rem(zq - n + parts - 1, parts - 1)
        return jnp.where(source, parts - 2 - n, head)

    adv_rel = cols - 1 - col

    def forward(z, p):
        got_z(z, p).wait_recv()
        for d in range(1, cols):
            copy_y(d, z, p).start()
        if p == nx - 1:
            copy_h(z, 0).start()
        if p == 0:
            copy_h(z, 1).start()

    def values_of(z, p):
        m = member(col, z)
        edge = bq[z].astype(F32)
        if p == 0:
            copy_h(z, 0).wait_recv()
        if p == nx - 1:
            copy_h(z, 1).wait_recv()
        grads = []
        for c in range(comps):
            u = p * comps + c
            at = (p + 1) * comps + c
            center = gq[m, at].astype(F32)
            gx = 0.5 * (gq[m, at + comps].astype(F32) - gq[m, at - comps].astype(F32))
            gy = 0.5 * (roll(center, -width) - roll(center, width))
            after = jnp.where(inner == width - 1, roll(edge, width - 2 - 2 * u), roll(center, -1))
            before = jnp.where(inner == 0, roll(edge, -2 * u), roll(center, 1))
            grads.append((gx, gy, 0.5 * (after - before)))

        def line(j, carry):
            rows = [jnp.broadcast_to(advf[p, d, pl.ds(j, 1), :], (nm, lanes)) for d in range(3)]
            start = pl.multiple_of(j * nm, nm)
            for c in range(comps):
                value = rows[0] * grads[c][0] + rows[1] * grads[c][1] + rows[2] * grads[c][2]
                vals[z, p * comps + c, pl.ds(start, nm), :] = value.astype(BF16)
            return carry

        lax.fori_loop(0, nm, line, 0, unroll=4)

    adv_rel = cols - 1 - col

    for p in planes:
        @pl.when(jnp.logical_not(source))
        def _():
            forward(other(0), p)
            if p == planes[0]:
                for t in range(parts - 2):
                    @pl.when(t < zq)
                    def _():
                        for k in planes:
                            copy_z(t, k).start()

        @pl.when(col != cols - 1)
        def _():
            got_y(adv_rel, parts - 1, p).wait_recv()

        for d in range(comps):
            advf[p, d] = gq[adv_block, (p + 1) * comps + d].astype(F32)
        values_of(zq, p)

        @pl.when(source)
        def _():
            forward(other(0), p)

        @pl.when(jnp.logical_not(tail))
        def _():
            forward(other(1), p)

    for n in range(parts - 1):
        got_b(other(n)).wait_recv()
        for p in planes:
            values_of(other(n), p)
            if n == 0:
                @pl.when(tail)
                def _():
                    forward(other(1), p)

                for k in range(2, parts - 1):
                    forward(other(k), p)

    for d in range(1, cols):
        for z in range(parts):
            def rest(d=d, z=z):
                for p in range(nx):
                    got_y(d, z, p).wait_recv()
            if z == parts - 1:
                pl.when(adv_rel != d)(rest)
            else:
                rest()

    for u in range(units):
        weight = wq[u // comps, 0:1, :]
        for t in range(NPANEL):
            for r in range(per_panel):
                raw = gq[plan_ref[1 + t] * per_panel + r, comps + u].astype(F32)
                first = (t * per_panel + r) * nm
                wts[u, first : first + nm, :] = (weight * raw).astype(BF16)

    def gemm(i):
        z = lax.rem(zq + 1 + i // SPLIT, parts)
        first = i % SPLIT * span
        left = jnp.concatenate([wts[u] for u in range(units)], axis=1)
        right = jnp.concatenate([vals[z, u, first : first + span] for u in range(units)], axis=1)
        part = lax.dot_general(left, right, (((1,), (1,)), ((), ())), preferred_element_type=F32)
        for s in range(spaces):
            acc[i, s % 2, s // 2] = part[s * own_rows : (s + 1) * own_rows]
        cbo[i] = acc[i, 1 - core].astype(BF16)
        copy_c(i).start()

    def stage_s(i):
        copy_c(i).wait_recv()
        for h in range(half):
            xo[i, h] = (acc[i, core, h] + crx[i, h].astype(F32)).astype(BF16)
        for d in range(1, half):
            copy_s(i, d).start()
        own[i] = acc[i, core, row] + crx[i, row].astype(F32)

    def total(i):
        value = own[i]
        for d in range(1, half):
            got_s(i, d).wait_recv()
            value = value + xi[i, d - 1].astype(F32)
        return value

    def stage_r(i):
        if i < steps - SPLIT:
            zo[i] = total(i).astype(BF16)
            copy_r(i).start()
        else:
            first = (i - steps + SPLIT) * span
            fin[:, first : first + span] = total(i)

    for i in range(steps + LAG_R):
        if i < steps:
            gemm(i)
        if LAG_S <= i < steps + LAG_S:
            stage_s(i - LAG_S)
        if i >= LAG_R:
            stage_r(i - LAG_R)

    for k in range(SPLIT):
        result = fin[:, k * span : (k + 1) * span]
        for n in range(parts - 1):
            copy_r(n * SPLIT + k).wait_recv()
            result = result + zi[n * SPLIT + k].astype(F32)
        fin[:, k * span : (k + 1) * span] = result
    for a in range(nm * nm // lanes):
        block = fin[:, a * lanes : (a + 1) * lanes]
        for e in range(lanes // nm):
            turned = pltpu.roll(block, lanes - e * nm, 1) if e else block
            out_ref[pl.ds(a * (lanes // nm) + e, own_rows, stride=nm), :] = turned[:, :nm]

    for t in range(parts):
        @pl.when(t != zq)
        def _():
            for p in range(nx):
                copy_z(t, p).wait_send()
    for d in range(1, parts):
        copy_b(d).wait_send()
    for z in range(parts):
        for d in range(1, cols):
            for p in range(nx):
                copy_y(d, z, p).wait_send()
        for side in range(2):
            copy_h(z, side).wait_send()
    for i in range(steps):
        copy_c(i).wait_send()
        for d in range(1, half):
            copy_s(i, d).wait_send()
        if i < steps - SPLIT:
            copy_r(i).wait_send()


def solution(mesh):
    nmode, spaces = mesh.shape["mode"], mesh.shape["space"]

    def local(modes, weights, plan):
        comps, nm, nx, cy, lanes = modes.shape
        parts, units = cy, comps * nx
        cols, half = nmode // parts, spaces // 2
        test_count = NPANEL * PANEL
        own_rows = test_count // spaces
        assert PANEL % nm == 0 and lanes % parts == 0 and 2 * units <= lanes // parts
        assert nmode % (2 * parts) == 0 and spaces % 2 == 0
        vm = pl.BlockSpec(memory_space=pltpu.VMEM)
        dma = pltpu.SemaphoreType.DMA
        steps = parts * SPLIT
        piece = (own_rows, nm * nm // SPLIT)
        pairs = max(half - 1, 1)
        out = pl.pallas_call(
            functools.partial(kernel, (nmode, spaces)),
            out_shape=jax.ShapeDtypeStruct((own_rows * nm, nm), F32),
            in_specs=[pl.BlockSpec(memory_space=pltpu.SMEM), vm, vm],
            out_specs=vm,
            scratch_shapes=[
                pltpu.VMEM((parts, units, nm, lanes), BF16),
                pltpu.VMEM((parts, nm, lanes), BF16),
                pltpu.VMEM((nmode, units + 2 * comps, nm, lanes), BF16),
                pltpu.VMEM((parts, nm, lanes), BF16),
                pltpu.VMEM((nx, 8, lanes), F32),
                pltpu.VMEM((nx, comps, nm, lanes), F32),
                pltpu.VMEM((units, test_count, lanes), BF16),
                pltpu.VMEM((parts, units, nm * nm, lanes), BF16),
                pltpu.VMEM((steps, 2, half) + piece, F32),
                pltpu.VMEM((steps, half) + piece, BF16),
                pltpu.VMEM((steps, half) + piece, BF16),
                pltpu.VMEM((steps,) + piece, F32),
                pltpu.VMEM((steps, half) + piece, BF16),
                pltpu.VMEM((steps, pairs) + piece, BF16),
                pltpu.VMEM((steps - SPLIT,) + piece, BF16),
                pltpu.VMEM((steps - SPLIT,) + piece, BF16),
                pltpu.VMEM((own_rows, nm * nm), F32),
                dma((parts, nx)), dma((parts, nx)), dma((parts - 1,)), dma((parts,)),
                dma((cols - 1, parts, nx)), dma((cols - 1, parts, nx)), dma((parts, 2)), dma((parts, 2)),
                dma((steps,)), dma((steps,)), dma((steps, pairs)), dma((steps, pairs)),
                dma((steps - SPLIT,)), dma((steps - SPLIT,)),
            ],
            compiler_params=pltpu.CompilerParams(
                collective_id=0, has_side_effects=True, vmem_limit_bytes=56 * 1024 * 1024),
        )(plan, modes, weights)
        return out.reshape(own_rows, nm, nm)

    in_specs = (P(None, "mode", "space", None, None), P("space", None, None), P())
    return jax.shard_map(local, mesh=mesh, in_specs=in_specs, out_specs=P("space", None, "mode"), check_vma=False)
```

time: 43.8 us -> 41.4 us (0.945)
  Pallas kernels: 41.8 us -> 39.4 us
    pallas_call x1, Pallas kernels: 41.8 us -> 39.4 us  [local(): pl.pallas_call(functools.partial(kernel, (nmode, spaces)), out_shape=jax....]
    reshape x1 -> x0, local copies, waits for them, and re-layouts: 1.87 us -> none  [local(): return out.reshape(own_rows, nm, nm)]
    unnamed x0 -> x1, local copies, waits for them, and re-layouts: none -> 1.87 us
where the time goes in v2:
time: 41.4 us; the launch traced here: 41.3 us
  Pallas kernels  39.4 us (95%)
  local copies, waits for them, and re-layouts  1.87 us (5%)
    pallas_call x1, Pallas kernels, local(): pl.pallas_call(functools.partial(kernel, (nmode, spaces)), out_shape=jax....  39.4 us
    unnamed x1, local copies, waits for them, and re-layouts  1.87 us

profile of v2, /device:TPU:0, one launch (start us, length us, event | category | flops | bytes accessed | tf_op | source)
XLA Modules:
  0.0 41.3 jit_solution(16542713667008074424)
XLA Ops:
  0.0 39.4 %shard_map.37 = f32[1024,32]{1,0:T(8,128)} custom-call(s32[3]{0:T(128)} %plan_ref.1, bf16[3,32,4,4,128]{4,3,2,1,0:T(4,128)(2,1)} %x_ref.1, f32[4,4,128]{2,1,0:T(4,128)} %weights_ref.1), custom_call_target="tpu_custom_call" | custom-call | tf_op jit(solution)/shard_map/pallas_call | solution.py:380
  39.4 1.9 %copy.5 = f32[32,32,32]{2,1,0:T(8,128)} copy(f32[32,32,32]{2,1,0:T(8,128)} %bitcast.1) | data formatting | bytes 262144

commit v3 on v2

--- a/solution.py
+++ b/solution.py
@@ -11,7 +11,7 @@
 NPANEL = 2
 SPLIT = 2
 LAG_S = 2
-LAG_R = 5
+LAG_R = 7
 MESH = pl.DeviceIdType.MESH
 F32 = jnp.float32
 BF16 = jnp.bfloat16
@@ -182,8 +182,6 @@
     for d in range(1, parts):
         copy_b(d).start()
 
-    tail = zq == 0
-
     def other(n):
         head = parts - 1 if n == 0 else lax.rem(zq - n + parts - 1, parts - 1)
         return jnp.where(source, parts - 2 - n, head)
@@ -232,13 +230,15 @@
     for p in planes:
         @pl.when(jnp.logical_not(source))
         def _():
-            forward(other(0), p)
-            if p == planes[0]:
-                for t in range(parts - 2):
-                    @pl.when(t < zq)
-                    def _():
-                        for k in planes:
-                            copy_z(t, k).start()
+            at = planes.index(p)
+            for k in planes[:2] if at == 0 else planes[at + 1 : at + 2]:
+                forward(other(0), k)
+                if k == planes[0]:
+                    for t in range(parts - 2):
+                        @pl.when(t < zq)
+                        def _():
+                            for r in planes:
+                                copy_z(t, r).start()
 
         @pl.when(col != cols - 1)
         def _():
@@ -251,21 +251,13 @@
         @pl.when(source)
         def _():
             forward(other(0), p)
-
-        @pl.when(jnp.logical_not(tail))
-        def _():
-            forward(other(1), p)
 
     for n in range(parts - 1):
         got_b(other(n)).wait_recv()
         for p in planes:
             values_of(other(n), p)
             if n == 0:
-                @pl.when(tail)
-                def _():
-                    forward(other(1), p)
-
-                for k in range(2, parts - 1):
+                for k in range(1, parts - 1):
                     forward(other(k), p)
 
     for d in range(1, cols):

time: 41.4 us -> 41 us (level)
  Pallas kernels: 39.4 us -> 38.9 us
    pallas_call x1, Pallas kernels: 39.4 us -> 38.9 us  [local(): pl.pallas_call(functools.partial(kernel, (nmode, spaces)), out_shape=jax....]
where the time goes in v3:
time: 41 us; the launch traced here: 40.8 us
  Pallas kernels  38.9 us (95%)
  local copies, waits for them, and re-layouts  1.87 us (5%)
    pallas_call x1, Pallas kernels, local(): pl.pallas_call(functools.partial(kernel, (nmode, spaces)), out_shape=jax....  38.9 us
    unnamed x1, local copies, waits for them, and re-layouts  1.87 us

profile of v3, /device:TPU:0, one launch (start us, length us, event | category | flops | bytes accessed | tf_op | source)
XLA Modules:
  0.0 40.8 jit_solution(6219388683115471612)
XLA Ops:
  0.0 38.9 %shard_map.37 = f32[1024,32]{1,0:T(8,128)} custom-call(s32[3]{0:T(128)} %plan_ref.1, bf16[3,32,4,4,128]{4,3,2,1,0:T(4,128)(2,1)} %x_ref.1, f32[4,4,128]{2,1,0:T(4,128)} %weights_ref.1), custom_call_target="tpu_custom_call" | custom-call | tf_op jit(solution)/shard_map/pallas_call | solution.py:372
  39.0 1.9 %copy.5 = f32[32,32,32]{2,1,0:T(8,128)} copy(f32[32,32,32]{2,1,0:T(8,128)} %bitcast.1) | data formatting | bytes 262144

commit v4 on v3

--- a/solution.py
+++ b/solution.py
@@ -304,13 +304,27 @@
             value = value + xi[i, d - 1].astype(F32)
         return value
 
+    def finish(k):
+        first = k * span
+        for n in range(parts - 1):
+            copy_r(n * SPLIT + k).wait_recv()
+        arrived = zi[k].astype(F32)
+        for n in range(1, parts - 1):
+            arrived = arrived + zi[n * SPLIT + k].astype(F32)
+        fin[:, first : first + span] = arrived
+        fin[:, first : first + span] += total(steps - SPLIT + k)
+        for a in range(first // lanes, (first + span) // lanes):
+            block = fin[:, a * lanes : (a + 1) * lanes]
+            for e in range(lanes // nm):
+                turned = pltpu.roll(block, lanes - e * nm, 1) if e else block
+                out_ref[pl.ds(a * (lanes // nm) + e, own_rows, stride=nm), :] = turned[:, :nm]
+
     def stage_r(i):
         if i < steps - SPLIT:
             zo[i] = total(i).astype(BF16)
             copy_r(i).start()
         else:
-            first = (i - steps + SPLIT) * span
-            fin[:, first : first + span] = total(i)
+            finish(i - steps + SPLIT)
 
     for i in range(steps + LAG_R):
         if i < steps:
@@ -319,18 +333,6 @@
             stage_s(i - LAG_S)
         if i >= LAG_R:
             stage_r(i - LAG_R)
-
-    for k in range(SPLIT):
-        result = fin[:, k * span : (k + 1) * span]
-        for n in range(parts - 1):
-            copy_r(n * SPLIT + k).wait_recv()
-            result = result + zi[n * SPLIT + k].astype(F32)
-        fin[:, k * span : (k + 1) * span] = result
-    for a in range(nm * nm // lanes):
-        block = fin[:, a * lanes : (a + 1) * lanes]
-        for e in range(lanes // nm):
-            turned = pltpu.roll(block, lanes - e * nm, 1) if e else block
-            out_ref[pl.ds(a * (lanes // nm) + e, own_rows, stride=nm), :] = turned[:, :nm]
 
     for t in range(parts):
         @pl.when(t != zq)

time: 41 us -> 40.8 us (level)
  no operation moved by 1% of the time
where the time goes in v4:
time: 40.8 us; the launch traced here: 40.6 us
  Pallas kernels  38.7 us (95%)
  local copies, waits for them, and re-layouts  1.87 us (5%)
    pallas_call x1, Pallas kernels, local(): pl.pallas_call(functools.partial(kernel, (nmode, spaces)), out_shape=jax....  38.7 us
    unnamed x1, local copies, waits for them, and re-layouts  1.87 us

profile of v4, /device:TPU:0, one launch (start us, length us, event | category | flops | bytes accessed | tf_op | source)
XLA Modules:
  0.0 40.6 jit_solution(4579560977399226295)
XLA Ops:
  0.0 38.7 %shard_map.37 = f32[1024,32]{1,0:T(8,128)} custom-call(s32[3]{0:T(128)} %plan_ref.1, bf16[3,32,4,4,128]{4,3,2,1,0:T(4,128)(2,1)} %x_ref.1, f32[4,4,128]{2,1,0:T(4,128)} %weights_ref.1), custom_call_target="tpu_custom_call" | custom-call | tf_op jit(solution)/shard_map/pallas_call | solution.py:374
  38.7 1.9 %copy.5 = f32[32,32,32]{2,1,0:T(8,128)} copy(f32[32,32,32]{2,1,0:T(8,128)} %bitcast.1) | data formatting | bytes 262144
